TPU v7x, 256 devices: a whole 4x4x8 slice. The times are simulated.
256 devices in a mesh: scen: 8 (over x, y_hi), rows: 32 (over z, y_lo, core).
Axes of the slice: x: 4, y: 4 (y_hi: 2, y_lo: 2; y = y_hi * 2 + y_lo), z: 8, core: 2. Of those that a mesh axis runs over, the one named last changes fastest.
Arguments:
- factor_rows: float32 [32, 16384, 1024], P('scen', 'rows'), may hold values from -1.5 to 1.5
- panel_factor: float32 [32, 1024, 512], P('scen'), may hold values from -0.03125 to 0.03125
- pivot_add: float32 [512, 512], replicated, may hold values from -1 to 4, as said below
- trailing: float32 [16384, 4096], P('rows', 'scen'), may hold values from -6 to 6
Outputs:
- panel: float32 [16384, 512], P('rows')
- updated: float32 [16384, 4096], P('rows', 'scen')
Inputs may be any that keep to these rules, and one draw needn't show every extreme that they name: `pivot_add`: symmetric positive definite; its diagonal lies between 1 and 3 and its off-diagonal entries are small.
All inputs are finite; a program needn't handle non-finite values.
Results may differ from a plain program's by a relative error of at most 0.0001.
Values sent between devices are 32-bit elements; how exact they have to be, the bound alone decides.
No kernel may reach another device: no remote copies, remote signals or barrier semaphores. Data moves between devices by JAX's collectives and lax.ppermute only.
A program may use at most 128 MiB of HBM per device.

v0:
```python
import jax
import jax.numpy as jnp
from jax import lax
from jax.sharding import PartitionSpec as P

exact_mode = lax.Precision.HIGHEST


def gram_matrix(stacked):
    return lax.dot_general(
        stacked,
        stacked,
        (((0,), (0,)), ((), ())),
        precision=exact_mode,
        preferred_element_type=jnp.float32,
    )


def solve_rows(factor_chol, right_rows):
    return lax.linalg.triangular_solve(
        factor_chol, right_rows, left_side=False, lower=True, transpose_a=True
    )


def per_device(factor_rows, panel_factor, pivot_add, trailing):
    groups = panel_factor.shape[0]
    depth = panel_factor.shape[1]
    width = panel_factor.shape[2]
    block_rows = factor_rows.shape[1]
    row_share = block_rows // lax.axis_size("scen")
    local_gram = gram_matrix(panel_factor.reshape(groups * depth, width))
    pivot_block, whole = lax.psum(
        (
            local_gram,
            jnp.einsum(
                "grk,gkp->rp",
                factor_rows,
                panel_factor,
                precision=exact_mode,
                preferred_element_type=jnp.float32,
            ),
        ),
        "scen",
    )
    factor_chol = jnp.linalg.cholesky(pivot_block + pivot_add)
    block = solve_rows(factor_chol, whole)
    own_solved = lax.dynamic_slice_in_dim(block, lax.axis_index("scen") * row_share, row_share, 0)
    tile_width = trailing.shape[1] // lax.axis_size("rows")
    product = jnp.dot(
        block,
        lax.all_gather(own_solved[:tile_width], "rows", axis=0, tiled=True).T,
        precision=exact_mode,
        preferred_element_type=jnp.float32,
    )
    return (block, trailing - product)


def solution(mesh):
    return jax.shard_map(
        per_device,
        mesh=mesh,
        in_specs=(P("scen", "rows", None), P("scen", None, None), P(), P("rows", "scen")),
        out_specs=(P("rows", None), P("rows", "scen")),
        check_vma=False,
    )
```

profile of v0, /device:TPU:1, one launch (start us, length us, event | category | flops | bytes accessed | tf_op | source)
XLA Modules:
  0.0 381.4 jit_solution(4032874341552375634)
XLA Ops:
  7.2 17.5 %convolution_bitcast_fusion = f32[512,512]{0,1:T(8,128)} fusion(f32[4,1024,512]{2,1,0:T(8,128)} %param.5), kind=kOutput, calls=%fused_computation.3 | convolution fusion | flops 12884901888 | bytes 9437184 | tf_op jit(solution)/shard_map/dot_general | solution.py:10
  24.8 14.7 %convolution_bitcast_fusion.1 = f32[512,512]{1,0:T(8,128)} fusion(f32[4,512,1024]{2,1,0:T(8,128)S(1)} %copy-done.1, f32[4,1024,512]{2,1,0:T(8,128)S(1)} %copy-done), kind=kOutput, calls=%fused_computation.4 | convolution fusion | flops 12884901888 | bytes 17825792 | tf_op jit(solution)/shard_map/grk,gkp->rp/dot_general | solution.py:35
  39.5 0.5 all-gather.2.cloned.1.call-start
  40.0 0.3 copy.13
  40.4 116.0 %all-reduce.4.cloned.1.call-done = (f32[512,512]{1,0:T(8,128)}, f32[512,512]{0,1:T(8,128)}) async-done(((f32[512,512]{1,0:T(8,128)}, f32[512,512]{0,1:T(8,128)}), (f32[512,512]{1,0:T(8,128)}, f32[512,512]{0,1:T(8,128)})) %all-reduce.4.cloned.1.call-update) | async-done | bytes 2097168 | tf_op jit(solution)/shard_map/psum | solution.py:32
  156.3 1.4 add.50
  157.7 0.3 copy.14
  158.1 0.2 fusion
  158.3 11.7 %cholesky.104 = f32[128,128]{1,0:T(8,128)S(1)} custom-call(f32[128,128]{1,0:T(8,128)S(1)} %cholesky.266), custom_call_target="Cholesky" | custom-call | tf_op jit(solution)/shard_map/jit(cholesky)/cholesky | solution.py:45
  170.1 9.8 %custom-call.30 = f32[1,128,128]{1,2,0:T(8,128)S(1)} custom-call(f32[1,128,128]{2,1,0:T(8,128)S(1)} %get-tuple-element.35), custom_call_target="InvertDiagBlocksLowerTriangular" | custom-call | tf_op jit(solution)/shard_map/jit(cholesky)/cholesky | solution.py:45
  179.9 0.1 cholesky.224
  180.0 0.3 constant_dynamic-update-slice_fusion.3
  180.4 0.3 convolution_subtract_fusion.4
  180.7 11.7 %cholesky.217 = f32[128,128]{1,0:T(8,128)S(1)} custom-call(f32[128,128]{1,0:T(8,128)S(1)} %cholesky.270), custom_call_target="Cholesky" | custom-call | tf_op jit(solution)/shard_map/jit(cholesky)/cholesky | solution.py:45
  192.5 9.9 %custom-call.31 = f32[1,128,128]{1,2,0:T(8,128)S(1)} custom-call(f32[1,128,128]{2,1,0:T(8,128)S(1)} %get-tuple-element.32), custom_call_target="InvertDiagBlocksLowerTriangular" | custom-call | tf_op jit(solution)/shard_map/jit(cholesky)/cholesky | solution.py:45
  202.4 0.3 convolution_dynamic-update-slice_fusion
  202.7 0.4 convolution_subtract_fusion.5
  203.1 11.7 %cholesky.238 = f32[128,128]{1,0:T(8,128)S(1)} custom-call(f32[128,128]{1,0:T(8,128)S(1)} %cholesky.275), custom_call_target="Cholesky" | custom-call | tf_op jit(solution)/shard_map/jit(cholesky)/cholesky | solution.py:45
  214.8 0.7 compare_reduce_fusion.1
  215.6 9.8 %custom-call.32 = f32[1,128,128]{1,2,0:T(8,128)S(1)} custom-call(f32[1,128,128]{2,1,0:T(8,128)S(1)} %get-tuple-element.29), custom_call_target="InvertDiagBlocksLowerTriangular" | custom-call | tf_op jit(solution)/shard_map/jit(cholesky)/cholesky | solution.py:45
  225.4 0.2 convolution_dynamic-update-slice_fusion.1
  225.6 0.4 convolution_subtract_fusion.6
  226.0 11.9 %cholesky.255 = f32[128,128]{1,0:T(8,128)S(1)} custom-call(f32[128,128]{1,0:T(8,128)S(1)} %convolution_subtract_fusion.6), custom_call_target="Cholesky" | custom-call | tf_op jit(solution)/shard_map/jit(cholesky)/cholesky | solution.py:45
  237.9 0.6 compare_reduce_fusion
  238.5 0.6 compare_reduce_fusion.2
  241.7 0.1 select_select_fusion
  241.9 10.4 %while.1 = (s32[]{:T(128)}, f32[512,512]{1,0:T(8,128)S(1)}, s32[4,2]{0,1:T(2,128)S(1)}, f32[4,128,128]{2,1,0:T(8,128)}, s32[]{:T(128)}) while((s32[]{:T(128)}, f32[512,512]{1,0:T(8,128)S(1)}, s32[4,2]{0,1:T(2,128)S(1)}, f32[4,128,128]{2,1,0:T(8,128)}, s32[]{:T(128)}) %tuple.33), condition=%wide.while_cond, body=%wide.while_body.sunk | while | flops 2 | bytes 132705 | solution.py:20
  242.0 0.5 fusion.42
  242.5 2.0 bitcast_dynamic-update-slice_fusion.2
  244.6 0.5 fusion.42
  245.1 2.0 bitcast_dynamic-update-slice_fusion.2
  247.2 0.5 fusion.42
  247.7 2.0 bitcast_dynamic-update-slice_fusion.2
  249.8 0.5 fusion.42
  250.3 2.0 bitcast_dynamic-update-slice_fusion.2
  252.3 40.1 %custom-call.33 = f32[4,128,128]{1,2,0:T(8,128)S(1)} custom-call(f32[4,128,128]{2,1,0:T(8,128)} %get-tuple-element.9), custom_call_target="InvertDiagBlocksLowerTriangular" | custom-call | tf_op jit(solution)/shard_map/triangular_solve | solution.py:20
  292.4 1.4 fusion.10
  293.8 1.5 convolution_subtract_fusion.2
  295.3 0.4 fusion.21
  295.8 1.9 convolution_subtract_fusion.1
  297.7 0.4 fusion.20
  298.1 2.4 convolution_subtract_fusion.3
  300.5 0.4 fusion.19
  301.0 0.1 constant_dynamic-slice_fusion.1
  301.2 0.7 copy.15
  301.9 1.3 copy.16
  303.2 65.4 %all-gather.2.cloned.1.call-done = f32[512,512]{1,0:T(8,128)} async-done(((f32[16,512]{1,0:T(8,128)}), f32[512,512]{1,0:T(8,128)}) %all-gather.2.cloned.1.call-update) | async-done | bytes 1048592 | tf_op jit(solution)/shard_map/all_gather | solution.py:51
  368.6 5.7 %convolution_subtract_fusion = f32[512,512]{1,0:T(8,128)} fusion(f32[512,512]{1,0:T(8,128)S(1)} %copy-done.3, f32[512,512]{1,0:T(8,128)} %all-gather.2.cloned.1.call-done, f32[512,128]{0,1:T(8,128)S(1)} %fusion.19, f32[512,128]{0,1:T(8,128)S(1)} %fusion.20, f32[512,128]{0,1:T(8,128)S(1)} %fusion.21, f32[512,128]{0,1:T(8,128)S(1)} %fusion.10), kind=kOutput, calls=%fused_computation.2 | convolution fusion | flops 1611661312 | bytes 4194304 | tf_op jit(solution)/shard_map/dot_general | solution.py:49
  (26 shorter events, 0.6 us)
Async XLA Ops:
  7.2 149.2 %all-reduce.4.cloned.1.call-start = ((), (), s32[]{:S(2)}) async-start(), calls=%async_computation.1 | async-start | bytes 4194304 | tf_op jit(solution)/shard_map/psum | solution.py:32
  7.2 17.5 %copy-start = (f32[4,1024,512]{2,1,0:T(8,128)S(1)}, f32[4,1024,512]{2,1,0:T(8,128)}, u32[]{:S(2)}) copy-start(f32[4,1024,512]{2,1,0:T(8,128)} %param.5) | copy-start | bytes 25165828
  7.2 17.5 %copy-start.1 = (f32[4,512,1024]{2,1,0:T(8,128)S(1)}, f32[4,512,1024]{2,1,0:T(8,128)}, u32[]{:S(2)}) copy-start(f32[4,512,1024]{2,1,0:T(8,128)} %param.4) | copy-start | bytes 25165828
  24.8 15.2 %copy-start.2 = (f32[512,512]{1,0:T(8,128)S(1)}, f32[512,512]{1,0:T(8,128)}, u32[]{:S(2)}) copy-start(f32[512,512]{1,0:T(8,128)} %param.6) | copy-start | bytes 3145732
  39.5 329.1 %all-gather.2.cloned.1.call-start = ((), (), s32[]{:S(2)}) async-start(), calls=%async_computation | async-start | bytes 1081344 | tf_op jit(solution)/shard_map/all_gather | solution.py:51
  180.3 188.3 %copy-start.3 = (f32[512,512]{1,0:T(8,128)S(1)}, f32[512,512]{1,0:T(8,128)}, u32[]{:S(2)}) copy-start(f32[512,512]{1,0:T(8,128)} %param.7) | copy-start | bytes 3145732
Sparse Core Ops, SparseCore 0:
  39.6 116.6 all-reduce.3
  302.1 66.5 all-gather.1
where the time goes:
time: 387 us; the launch traced here: 381 us
  waiting for transfers between devices  181 us (47%)
  other arithmetic  121 us (31%)
  matrix products  48.2 us (12%)
  between operations  17.1 us (4%)
  local copies, waits for them, and re-layouts  13.4 us (3%)
    psum x1, waiting for transfers between devices, per_device(): lax.psum((local_gram, jnp.einsum('grk,gkp->rp', factor_rows, panel_factor...  116 us
    another operation x14, other arithmetic, per_device(): factor_chol = jnp.linalg.cholesky(pivot_block + pivot_add)  78.7 us
    all_gather x1, waiting for transfers between devices, per_device(): lax.all_gather(own_solved[:tile_width], 'rows', axis=0, tiled=True)  65.4 us
    another operation x4, other arithmetic, solve_rows(): lax.linalg.triangular_solve(factor_chol, right_rows, left_side=False, low...  40.3 us
    dot_general x1, matrix products, gram_matrix(): lax.dot_general(stacked, stacked, (((0,), (0,)), ((), ())), precision=exa...  17.5 us
    dot_general x1, matrix products, per_device(): jnp.einsum('grk,gkp->rp', factor_rows, panel_factor, precision=exact_mode...  14.7 us
    another operation x12, local copies, waits for them, and re-layouts  10.4 us
    another operation x7, matrix products, solve_rows(): lax.linalg.triangular_solve(factor_chol, right_rows, left_side=False, low...  8.5 us
  transfers between devices with their start and end apart: 2, of which 2 were waited for; matrix products, arithmetic and copies ran while one was open for 0% of the time, Pallas kernels for 0%

commit v1 on v0

--- a/solution.py
+++ b/solution.py
@@ -4,6 +4,13 @@
 from jax.sharding import PartitionSpec as P
 
 exact_mode = lax.Precision.HIGHEST
+
+
+def all_by_exchange(x, name, along):
+    size = lax.axis_size(name)
+    shards = jnp.stack([x for _ in range(size)])
+    shards = lax.all_to_all(shards, name, split_axis=0, concat_axis=0)
+    return jnp.concatenate(shards, axis=along)
 
 
 def gram_matrix(stacked):
@@ -48,7 +55,7 @@
     tile_width = trailing.shape[1] // lax.axis_size("rows")
     product = jnp.dot(
         block,
-        lax.all_gather(own_solved[:tile_width], "rows", axis=0, tiled=True).T,
+        all_by_exchange(own_solved[:tile_width], "rows", 0).T,
         precision=exact_mode,
         preferred_element_type=jnp.float32,
     )

time: 387 us -> 358 us (0.925)
  waiting for transfers between devices: 181 us -> 143 us
  starting transfers between devices: 0.55 us -> 11.3 us
    all_gather x1 -> x0, waiting for transfers between devices: 65.4 us -> none  [per_device(): lax.all_gather(own_solved[:tile_width], 'rows', axis=0, tiled=True)]
    all_to_all x0 -> x1, waiting for transfers between devices: none -> 26.8 us  [all_by_exchange(): shards = lax.all_to_all(shards, name, split_axis=0, concat_axis=0)]
    all_to_all x0 -> x1, starting transfers between devices: none -> 11.2 us  [all_by_exchange(): shards = lax.all_to_all(shards, name, split_axis=0, concat_axis=0)]
    another operation x12 -> x13, local copies, waits for them, and re-layouts: 10.4 us -> 9.03 us
where the time goes in v1:
time: 358 us; the launch traced here: 352 us
  waiting for transfers between devices  143 us (40%)
  other arithmetic  120 us (34%)
  matrix products  48.7 us (14%)
  between operations  17.1 us (5%)
  local copies, waits for them, and re-layouts  11.4 us (3%)
  starting transfers between devices  11.3 us (3%)
    psum x1, waiting for transfers between devices, per_device(): lax.psum((local_gram, jnp.einsum('grk,gkp->rp', factor_rows, panel_factor...  116 us
    another operation x14, other arithmetic, per_device(): factor_chol = jnp.linalg.cholesky(pivot_block + pivot_add)  78.8 us
    another operation x4, other arithmetic, solve_rows(): lax.linalg.triangular_solve(factor_chol, right_rows, left_side=False, low...  39.5 us
    all_to_all x1, waiting for transfers between devices, all_by_exchange(): shards = lax.all_to_all(shards, name, split_axis=0, concat_axis=0)  26.8 us
    dot_general x1, matrix products, gram_matrix(): lax.dot_general(stacked, stacked, (((0,), (0,)), ((), ())), precision=exa...  17.5 us
    dot_general x1, matrix products, per_device(): jnp.einsum('grk,gkp->rp', factor_rows, panel_factor, precision=exact_mode...  15.1 us
    all_to_all x1, starting transfers between devices, all_by_exchange(): shards = lax.all_to_all(shards, name, split_axis=0, concat_axis=0)  11.2 us
    another operation x7, matrix products, solve_rows(): lax.linalg.triangular_solve(factor_chol, right_rows, left_side=False, low...  8.49 us
  transfers between devices with their start and end apart: 2, of which 2 were waited for; matrix products, arithmetic and copies ran while one was open for 0% of the time, Pallas kernels for 0%

profile of v1, /device:TPU:1, one launch (start us, length us, event | category | flops | bytes accessed | tf_op | source)
XLA Modules:
  0.0 351.7 jit_solution(1069825765688010520)
XLA Ops:
  7.2 17.5 %convolution_bitcast_fusion = f32[512,512]{0,1:T(8,128)} fusion(f32[4,1024,512]{2,1,0:T(8,128)} %param.5), kind=kOutput, calls=%fused_computation.3 | convolution fusion | flops 12884901888 | bytes 9437184 | tf_op jit(solution)/shard_map/dot_general | solution.py:17
  24.8 15.1 %convolution_bitcast_fusion.1 = f32[512,512]{1,0:T(8,128)} fusion(f32[4,512,1024]{2,1,0:T(8,128)S(1)} %copy-done.1, f32[4,1024,512]{2,1,0:T(8,128)S(1)} %copy-done), kind=kOutput, calls=%fused_computation.4 | convolution fusion | flops 12884901888 | bytes 17825792 | tf_op jit(solution)/shard_map/grk,gkp->rp/dot_general | solution.py:42
  39.9 0.3 copy.8
  40.3 116.5 %all-reduce.4.cloned.1.call-done = (f32[512,512]{1,0:T(8,128)}, f32[512,512]{0,1:T(8,128)}) async-done(((f32[512,512]{1,0:T(8,128)}, f32[512,512]{0,1:T(8,128)}), (f32[512,512]{1,0:T(8,128)}, f32[512,512]{0,1:T(8,128)})) %all-reduce.4.cloned.1.call-update) | async-done | bytes 2097168 | tf_op jit(solution)/shard_map/psum | solution.py:39
  156.8 1.4 add.50
  158.2 0.3 copy.9
  158.5 0.2 fusion
  158.8 11.7 %cholesky.104 = f32[128,128]{1,0:T(8,128)S(1)} custom-call(f32[128,128]{1,0:T(8,128)S(1)} %cholesky.266), custom_call_target="Cholesky" | custom-call | tf_op jit(solution)/shard_map/jit(cholesky)/cholesky | solution.py:52
  170.5 9.8 %custom-call.30 = f32[1,128,128]{1,2,0:T(8,128)S(1)} custom-call(f32[1,128,128]{2,1,0:T(8,128)S(1)} %get-tuple-element.33), custom_call_target="InvertDiagBlocksLowerTriangular" | custom-call | tf_op jit(solution)/shard_map/jit(cholesky)/cholesky | solution.py:52
  180.3 0.1 cholesky.224
  180.5 0.3 constant_dynamic-update-slice_fusion.3
  180.8 0.3 convolution_subtract_fusion.4
  181.1 11.7 %cholesky.217 = f32[128,128]{1,0:T(8,128)S(1)} custom-call(f32[128,128]{1,0:T(8,128)S(1)} %cholesky.270), custom_call_target="Cholesky" | custom-call | tf_op jit(solution)/shard_map/jit(cholesky)/cholesky | solution.py:52
  192.9 10.0 %custom-call.31 = f32[1,128,128]{1,2,0:T(8,128)S(1)} custom-call(f32[1,128,128]{2,1,0:T(8,128)S(1)} %get-tuple-element.30), custom_call_target="InvertDiagBlocksLowerTriangular" | custom-call | tf_op jit(solution)/shard_map/jit(cholesky)/cholesky | solution.py:52
  202.9 0.3 convolution_dynamic-update-slice_fusion
  203.1 0.4 convolution_subtract_fusion.5
  203.5 11.7 %cholesky.238 = f32[128,128]{1,0:T(8,128)S(1)} custom-call(f32[128,128]{1,0:T(8,128)S(1)} %cholesky.275), custom_call_target="Cholesky" | custom-call | tf_op jit(solution)/shard_map/jit(cholesky)/cholesky | solution.py:52
  215.3 0.7 compare_reduce_fusion.1
  216.0 9.8 %custom-call.32 = f32[1,128,128]{1,2,0:T(8,128)S(1)} custom-call(f32[1,128,128]{2,1,0:T(8,128)S(1)} %get-tuple-element.27), custom_call_target="InvertDiagBlocksLowerTriangular" | custom-call | tf_op jit(solution)/shard_map/jit(cholesky)/cholesky | solution.py:52
  225.8 0.2 convolution_dynamic-update-slice_fusion.1
  226.0 0.4 convolution_subtract_fusion.6
  226.4 11.9 %cholesky.255 = f32[128,128]{1,0:T(8,128)S(1)} custom-call(f32[128,128]{1,0:T(8,128)S(1)} %convolution_subtract_fusion.6), custom_call_target="Cholesky" | custom-call | tf_op jit(solution)/shard_map/jit(cholesky)/cholesky | solution.py:52
  238.4 0.6 compare_reduce_fusion
  239.0 0.6 compare_reduce_fusion.2
  242.2 0.1 select_select_fusion
  242.3 8.0 %while.1 = (s32[]{:T(128)}, f32[512,512]{1,0:T(8,128)S(1)}, s32[4,2]{0,1:T(2,128)S(1)}, f32[4,128,128]{2,1,0:T(8,128)S(1)}, s32[]{:T(128)}) while((s32[]{:T(128)}, f32[512,512]{1,0:T(8,128)S(1)}, s32[4,2]{0,1:T(2,128)S(1)}, f32[4,128,128]{2,1,0:T(8,128)S(1)}, s32[]{:T(128)}) %tuple.32), condition=%wide.while_cond, body=%wide.while_body.sunk | while | flops 2 | bytes 131181 | solution.py:27
  242.4 0.5 fusion.42
  242.9 1.4 bitcast_dynamic-update-slice_fusion.2
  244.4 0.5 fusion.42
  244.9 1.4 bitcast_dynamic-update-slice_fusion.2
  246.4 0.5 fusion.42
  246.9 1.4 bitcast_dynamic-update-slice_fusion.2
  248.4 0.5 fusion.42
  248.9 1.4 bitcast_dynamic-update-slice_fusion.2
  250.3 39.3 %custom-call.33 = f32[4,128,128]{1,2,0:T(8,128)S(1)} custom-call(f32[4,128,128]{2,1,0:T(8,128)S(1)} %get-tuple-element.9), custom_call_target="InvertDiagBlocksLowerTriangular" | custom-call | tf_op jit(solution)/shard_map/triangular_solve | solution.py:27
  289.7 1.4 fusion.10
  291.0 1.5 convolution_subtract_fusion.2
  292.6 0.4 fusion.21
  293.0 1.9 convolution_subtract_fusion.1
  295.0 0.4 fusion.20
  295.4 2.4 convolution_subtract_fusion.3
  297.8 0.4 fusion.19
  298.3 0.1 constant_dynamic-slice_fusion.1
  298.5 1.1 stack.2
  299.6 11.2 %all-to-all-start = ((f32[32,16,512]{2,1,0:T(8,128)}), f32[32,16,512]{2,1,0:T(8,128)S(1)}, u32[]{:S(2)}, u32[]{:S(2)}) async-start(f32[32,16,512]{2,1,0:T(8,128)} %stack.2), calls=%async_computation | async-start | bytes 2097152 | tf_op jit(solution)/shard_map/all_to_all | solution.py:12
  310.9 1.3 copy.11
  312.2 26.8 %all-to-all-done = f32[32,16,512]{2,1,0:T(8,128)S(1)} async-done(((f32[32,16,512]{2,1,0:T(8,128)}), f32[32,16,512]{2,1,0:T(8,128)S(1)}, u32[]{:S(2)}, u32[]{:S(2)}) %all-to-all-start) | async-done | bytes 1048608 | tf_op jit(solution)/shard_map/all_to_all | solution.py:12
  339.0 5.7 %convolution_subtract_fusion = f32[512,512]{1,0:T(8,128)} fusion(f32[512,512]{1,0:T(8,128)} %param.7, f32[512,512]{1,0:T(8,128)S(1)} %bitcast.58, f32[512,128]{0,1:T(8,128)S(1)} %fusion.19, f32[512,128]{0,1:T(8,128)S(1)} %fusion.20, f32[512,128]{0,1:T(8,128)S(1)} %fusion.21, f32[512,128]{0,1:T(8,128)S(1)} %fusion.10), kind=kOutput, calls=%fused_computation.2 | convolution fusion | flops 1611661312 | bytes 4194304 | tf_op jit(solution)/shard_map/dot_general | solution.py:56
  (24 shorter events, 0.7 us)
Async XLA Ops:
  7.2 149.6 %all-reduce.4.cloned.1.call-start = ((), (), s32[]{:S(2)}) async-start(), calls=%async_computation.1 | async-start | bytes 4194304 | tf_op jit(solution)/shard_map/psum | solution.py:39
  7.2 17.5 %copy-start = (f32[4,1024,512]{2,1,0:T(8,128)S(1)}, f32[4,1024,512]{2,1,0:T(8,128)}, u32[]{:S(2)}) copy-start(f32[4,1024,512]{2,1,0:T(8,128)} %param.5) | copy-start | bytes 25165828
  7.2 17.5 %copy-start.1 = (f32[4,512,1024]{2,1,0:T(8,128)S(1)}, f32[4,512,1024]{2,1,0:T(8,128)}, u32[]{:S(2)}) copy-start(f32[4,512,1024]{2,1,0:T(8,128)} %param.4) | copy-start | bytes 25165828
  24.8 15.2 %copy-start.2 = (f32[512,512]{1,0:T(8,128)S(1)}, f32[512,512]{1,0:T(8,128)}, u32[]{:S(2)}) copy-start(f32[512,512]{1,0:T(8,128)} %param.6) | copy-start | bytes 3145732
  299.6 39.3 %all-to-all-start = ((f32[32,16,512]{2,1,0:T(8,128)}), f32[32,16,512]{2,1,0:T(8,128)S(1)}, u32[]{:S(2)}, u32[]{:S(2)}) async-start(f32[32,16,512]{2,1,0:T(8,128)} %stack.2), calls=%async_computation | async-start | bytes 2097152 | tf_op jit(solution)/shard_map/all_to_all | solution.py:12
Sparse Core Ops, SparseCore 0:
  40.0 116.6 all-reduce.3
